TPU v7x, 32 devices: a whole 2x2x4 slice. The times are simulated.
32 devices in a mesh: slab: 8 (over z, y), grp: 4 (over x, core).
Axes of the slice: x: 2, y: 2, z: 4, core: 2. Of those that a mesh axis runs over, the one named last changes fastest.
Arguments:
- potential: bfloat16 [64, 8, 1024], P('slab'), may hold values from -3 to 3
- coefficients: bfloat16 [128, 16, 8, 1024], P(('slab', 'grp')), may hold values from -1 to 1
- box_center: int32 [128], replicated, may hold values from 0 to 63, as said below
- box_extent: int32 [128], replicated, may hold values from 8 to 16
Outputs:
- margin: float32 [128, 80], P(('slab', 'grp'))
- hamiltonian: float32 [128, 80], P(('slab', 'grp'))
Inputs may be any that keep to these rules, and one draw needn't show every extreme that they name: `box_center`: function b's centre lies among the 8 planes of slab b // 16, that is from (8 * (b // 16)) on.
All inputs are finite; a program needn't handle non-finite values.
Results may differ from a plain program's by a relative error of at most 0.0003.
Values may be sent and summed in bfloat16 or wider, within the bound.
A program may use at most 64 MiB of HBM per device.

v0:
```python
import jax
import jax.numpy as jnp
from jax import lax
from jax.sharding import PartitionSpec as P

COMP = 8
CX = 32
CY = 32


def with_halo(value, sides, width):
    for axis, dim in sides:
        size, length = (lax.axis_size(axis), value.shape[dim])
        up = [(i, (i + 1) % size) for i in range(size)]
        down = [(j, i) for i, j in up]
        last = lax.slice_in_dim(value, length - width, length, axis=dim)
        initial = lax.slice_in_dim(value, 0, width, axis=dim)
        before = lax.ppermute(last, axis, up)
        after = lax.ppermute(initial, axis, down)
        value = jnp.concatenate([before, value, after], axis=dim)
    return value


def shifted(value, axis, steps):
    count = lax.axis_size(axis)
    pairs = [(source, (source + steps) % count) for source in range(count)]
    return lax.ppermute(value, axis, pairs)


def haar_signs():
    row_ids = jnp.arange(COMP, dtype=jnp.int32)[:, None]
    col_ids = jnp.arange(COMP, dtype=jnp.int32)[None, :]
    common = jnp.bitwise_and(row_ids, col_ids)
    parity = (common % 2 + common // 2 % 2 + common // 4 % 2) % 2
    return (1 - 2 * parity).astype(jnp.float32)


def laplace_plane():
    cells = jnp.arange(CX * CY, dtype=jnp.int32)
    first_x = (cells // CY)[:, None]
    second_x = (cells // CY)[None, :]
    first_y = (cells % CY)[:, None]
    second_y = (cells % CY)[None, :]
    step_x = jnp.abs(first_x - second_x)
    step_y = jnp.abs(first_y - second_y)
    beside = (step_x == 1) & (first_y == second_y) | (step_y == 1) & (first_x == second_x)
    same_cell = (first_x == second_x) & (first_y == second_y)
    return jnp.where(same_cell, 2.0, jnp.where(beside, -0.5, 0.0)).astype(jnp.bfloat16)


def apply_hamiltonian(orbital, pot_box, inside):
    cell_count = orbital.shape[3]
    plane_term = jnp.dot(
        orbital.reshape(-1, cell_count), laplace_plane(), preferred_element_type=jnp.float32
    ).reshape(orbital.shape)
    padded = jnp.pad(orbital, ((0, 0), (1, 1), (0, 0), (0, 0)))
    depth_term = orbital.astype(jnp.float32) - 0.5 * (
        padded[:, :-2].astype(jnp.float32) + padded[:, 2:].astype(jnp.float32)
    )
    haar_table = haar_signs()
    fine_values = jnp.einsum(
        "kc,npcx->npkx",
        haar_table.astype(jnp.bfloat16),
        orbital,
        preferred_element_type=jnp.float32,
    )
    potential_term = (
        jnp.einsum(
            "kc,npkx->npcx",
            haar_table,
            pot_box.astype(jnp.float32) * fine_values,
            precision=lax.Precision.HIGHEST,
        )
        / COMP
    )
    return jnp.where(inside, plane_term + depth_term + potential_term, 0.0).astype(jnp.bfloat16)


def place_planes(starts, frame_depth, tile_data):
    source = jnp.arange(tile_data.shape[1], dtype=jnp.int32)
    target = jnp.arange(frame_depth, dtype=jnp.int32)
    onehot = (starts[:, None, None] + source[None, None, :] == target[None, :, None]).astype(
        jnp.bfloat16
    )
    placed = jnp.einsum("nqp,npcx->nqcx", onehot, tile_data, preferred_element_type=jnp.float32)
    return placed.astype(jnp.bfloat16)


def into_band(block_rows, offset, members):
    return jnp.pad(block_rows, ((0, 0), (offset * members, (2 - offset) * members)))


def local(potential, coefficients, box_center, box_extent):
    slab_index = lax.axis_index("slab")
    group_index = lax.axis_index("grp")
    groups = lax.axis_size("grp")
    per_device = coefficients.shape[0]
    box_depth = coefficients.shape[1]
    slab_depth = potential.shape[0]
    rim_depth = box_depth // 2
    frame_depth = slab_depth + box_depth
    members = groups * per_device
    first_row = (slab_index * groups + group_index) * per_device
    centers = lax.dynamic_slice_in_dim(box_center, first_row, per_device)
    extents = lax.dynamic_slice_in_dim(box_extent, first_row, per_device)
    frame_starts = centers - slab_index * slab_depth - extents // 2 + rim_depth
    planes = jnp.arange(box_depth, dtype=jnp.int32)
    inside = (planes[None, :] < extents[:, None])[:, :, None, None]
    orbital = jnp.where(inside, coefficients, jnp.zeros((), jnp.bfloat16))
    pot_frame = with_halo(potential, (("slab", 0),), rim_depth)
    padded_pot = jnp.pad(pot_frame, ((0, box_depth), (0, 0), (0, 0)))

    def cut_box(start_at):
        return lax.dynamic_slice_in_dim(padded_pot, start_at, box_depth, 0)

    pot_box = jax.vmap(cut_box)(frame_starts)
    applied = apply_hamiltonian(orbital, pot_box, inside)
    frame_orbital = place_planes(frame_starts, frame_depth, orbital)
    frame_applied = place_planes(frame_starts, frame_depth, applied)
    got_orbital, got_applied = (
        lax.all_to_all(frame_orbital, "grp", split_axis=3, concat_axis=0, tiled=True),
        lax.all_to_all(frame_applied, "grp", split_axis=3, concat_axis=0, tiled=True),
    )
    middle_orbital = got_orbital[:, rim_depth : rim_depth + slab_depth]
    middle_applied = got_applied[:, rim_depth : rim_depth + slab_depth]
    lower_set = None
    upper_set = None
    for direction in (1, -1):
        if direction == 1:
            sent_orbital = got_orbital[:, rim_depth + slab_depth :]
            sent_applied = got_applied[:, rim_depth + slab_depth :]
        else:
            sent_orbital = got_orbital[:, :rim_depth]
            sent_applied = got_applied[:, :rim_depth]
        came_orbital, came_applied = shifted((sent_orbital, sent_applied), "slab", direction)
        placed_pair = (came_orbital, came_applied)
        if direction == 1:
            lower_set = placed_pair
        else:
            upper_set = placed_pair
    tile_orbital = jnp.concatenate([lower_set[0], middle_orbital, upper_set[0]], axis=0)
    tile_applied = jnp.concatenate([lower_set[1], middle_applied, upper_set[1]], axis=0)
    flat_orbital = tile_orbital.reshape(tile_orbital.shape[0], -1)
    flat_applied = tile_applied.reshape(tile_applied.shape[0], -1)
    contract = (((1,), (1,)), ((), ()))
    part_margin = lax.dot_general(
        flat_orbital, flat_orbital, contract, preferred_element_type=jnp.float32
    )
    part_ham = lax.dot_general(
        flat_applied, flat_orbital, contract, preferred_element_type=jnp.float32
    )
    total_margin = into_band(part_margin[members : 2 * members], 1, members)
    total_ham = into_band(part_ham[members : 2 * members], 1, members)
    for direction in (1, -1):
        if direction == 1:
            sent_margin = part_margin[2 * members :]
            sent_ham = part_ham[2 * members :]
        else:
            sent_margin = part_margin[:members]
            sent_ham = part_ham[:members]
        came_margin, came_ham = shifted((sent_margin, sent_ham), "slab", direction)
        offset = 0 if direction == 1 else 2
        total_margin = total_margin + into_band(came_margin, offset, members)
        total_ham = total_ham + into_band(came_ham, offset, members)
    margin, hamiltonian = (
        lax.psum_scatter(total_margin, "grp", scatter_dimension=0, tiled=True),
        lax.psum_scatter(total_ham, "grp", scatter_dimension=0, tiled=True),
    )
    return (margin, hamiltonian)


def solution(mesh):
    return jax.shard_map(
        local,
        mesh=mesh,
        in_specs=(P("slab", None, None), P(("slab", "grp"), None, None, None), P(), P()),
        out_specs=(P(("slab", "grp"), None), P(("slab", "grp"), None)),
        check_vma=False,
    )
```

profile of v0, /device:TPU:0, one launch (start us, length us, event | category | flops | bytes accessed | tf_op | source)
XLA Modules:
  0.0 191.3 jit_solution(1780533823639298639)
XLA Ops:
  0.6 3.0 %collective-permute-start.4 = (bf16[8,8,1024]{2,1,0:T(8,128)(2,1)}, bf16[8,8,1024]{2,1,0:T(8,128)(2,1)S(1)}, u32[]{:S(2)}, u32[]{:S(2)}) collective-permute-start(bf16[8,8,1024]{2,1,0:T(8,128)(2,1)} %param.4), channel_id=1, source_target_pairs={{0,4},{4,8},{8,12},{12,16},{16,20},{20,24},{24,28},{28,0},{1,5},{5... | collective-permute-start | bytes 393224 | tf_op jit(solution)/shard_map/ppermute | solution.py:18
  3.7 3.1 %collective-permute-start.5 = (bf16[8,8,1024]{2,1,0:T(8,128)(2,1)}, bf16[8,8,1024]{2,1,0:T(8,128)(2,1)S(1)}, u32[]{:S(2)}, u32[]{:S(2)}) collective-permute-start(bf16[8,8,1024]{2,1,0:T(8,128)(2,1)} %param.4), channel_id=1, source_target_pairs={{4,0},{8,4},{12,8},{16,12},{20,16},{24,20},{28,24},{0,28},{5,1},{9... | collective-permute-start | bytes 393224 | tf_op jit(solution)/shard_map/ppermute | solution.py:19
  10.0 12.2 %copy.11 = bf16[4,24,8,1024]{1,2,0,3:T(8,128)(2,1)} copy(bf16[4,24,8,1024]{3,1,2,0:T(8,128)(2,1)S(1)} %convolution_convert_fusion.1) | data formatting | bytes 3145728 | tf_op jit(solution)/shard_map/convert_element_type | solution.py:86
  22.2 13.3 %reshape.116 = bf16[4,2,98304]{2,1,0:T(2,128)(2,1)} reshape(bf16[1024,4,8,24]{3,2,1,0:T(8,128)(2,1)} %bitcast.55) | data formatting | bytes 3145728
  35.5 4.5 %all-to-all-start = ((bf16[4,2,98304]{2,1,0:T(2,128)(2,1)}), bf16[4,2,98304]{2,1,0:T(2,128)(2,1)}, u32[]{:S(2)}, u32[]{:S(2)}) async-start(bf16[4,2,98304]{2,1,0:T(2,128)(2,1)} %reshape.116), calls=%async_computation | async-start | bytes 3145728 | tf_op jit(solution)/shard_map/all_to_all | solution.py:121
  40.1 5.2 %fusion.2 = f32[4,16,8,1024]{3,2,1,0:T(8,128)} fusion(bf16[4,16,8,1024]{3,2,1,0:T(8,128)(2,1)S(1)} %broadcast_select_fusion, s32[1024]{0:T(1024)S(1)} %get-tuple-element.19, s32[1024]{0:T(1024)S(1)} %get-tuple-element.20), kind=kOutput, calls=%fused_computation.9 | convolution fusion | flops 1089470464 | bytes 3153920 | tf_op jit(solution)/shard_map/dot_general | solution.py:53
  47.1 2.7 %gather_fusion = bf16[4,16,8,1024]{3,2,1,0:T(8,128)(2,1)} fusion(bf16[40,8,1024]{2,1,0:T(8,128)(2,1)} %fusion.31, s32[4]{0:T(128)S(1)} %get-tuple-element.4), kind=kCustom, calls=%fused_computation | custom fusion | bytes 2097200 | tf_op jit(solution)/shard_map/vmap()/gather | solution.py:114
  49.7 4.4 %fusion.5 = bf16[4,16,8,1024]{3,2,1,0:T(8,128)(2,1)S(1)} fusion(f32[4,16,8,1024]{3,2,1,0:T(8,128)} %fusion.2, bf16[4,16,8,1024]{3,2,1,0:T(8,128)(2,1)S(1)} %broadcast_select_fusion, f32[4,16,1024,8]{2,3,1,0:T(8,128)S(1)} %fusion.59, bf16[4,16,8,1024]{3,2,1,0:T(8,128)(2,1)} %gather_fusion, pred[4,16]{1,0:T(4,128)(4,1)S(1)} %iota_compare_fusion.2), kind=kOutput, calls=%fused_computation.12 | convolution fusion | flops 57151744 | bytes 7340096 | tf_op jit(solution)/shard_map/kc,npkx->npcx/dot_general | solution.py:68
  55.1 12.2 %copy.14 = bf16[4,24,8,1024]{1,2,0,3:T(8,128)(2,1)} copy(bf16[4,24,8,1024]{3,1,2,0:T(8,128)(2,1)S(1)} %convolution_convert_fusion) | data formatting | bytes 3145728 | tf_op jit(solution)/shard_map/convert_element_type | solution.py:86
  67.4 13.3 %reshape.118 = bf16[4,2,98304]{2,1,0:T(2,128)(2,1)} reshape(bf16[1024,4,8,24]{3,2,1,0:T(8,128)(2,1)} %bitcast.56) | data formatting | bytes 3145728
  80.6 3.8 %all-to-all-start.1 = ((bf16[4,2,98304]{2,1,0:T(2,128)(2,1)}), bf16[4,2,98304]{2,1,0:T(2,128)(2,1)S(1)}, u32[]{:S(2)}, u32[]{:S(2)}) async-start(bf16[4,2,98304]{2,1,0:T(2,128)(2,1)} %reshape.118), calls=%async_computation.1 | async-start | bytes 3145728 | tf_op jit(solution)/shard_map/all_to_all | solution.py:122
  84.4 14.1 %reshape.117 = bf16[1024,4,8,24]{3,2,1,0:T(8,128)(2,1)} reshape(bf16[4,2,98304]{2,1,0:T(2,128)(2,1)} %all-to-all-done) | data formatting | bytes 3145728
  98.5 12.8 %copy.12 = bf16[4,24,8,4,256]{4,0,3,2,1:T(4,128)(2,1)} copy(bf16[4,24,8,4,256]{1,2,0,4,3:T(8,128)(2,1)} %bitcast.57) | data formatting | bytes 3145728 | tf_op jit(solution)/shard_map/all_to_all | solution.py:121
  111.2 2.4 %all_to_all.29 = bf16[16,24,8,256]{3,0,2,1:T(8,128)(2,1)S(1)} reshape(bf16[4,4,24,8,256]{4,1,0,3,2:T(4,128)(2,1)} %bitcast.59) | data formatting | bytes 3145728 | tf_op jit(solution)/shard_map/all_to_all | solution.py:121
  114.8 4.7 %collective-permute-start.1 = (bf16[16,8,8,256]{3,0,2,1:T(8,128)(2,1)}, bf16[16,8,8,256]{3,0,2,1:T(8,128)(2,1)}, u32[]{:S(2)}, u32[]{:S(2)}) collective-permute-start(bf16[16,8,8,256]{3,0,2,1:T(8,128)(2,1)} %get-tuple-element.11), channel_id=1, source_target_pairs={{0,28},{4,0},{8,4},{12,8},{16,12},{20,16},{24,20},{28,24},{1,29},{... | collective-permute-start | bytes 1572872 | tf_op jit(solution)/shard_map/ppermute | solution.py:27
  119.5 13.4 %reshape.119 = bf16[1024,4,8,24]{3,2,1,0:T(8,128)(2,1)} reshape(bf16[4,2,98304]{2,1,0:T(2,128)(2,1)S(1)} %all-to-all-done.1) | data formatting | bytes 3145728
  132.9 12.3 %copy.15 = bf16[4,24,8,4,256]{4,0,3,2,1:T(4,128)(2,1)S(1)} copy(bf16[4,24,8,4,256]{1,2,0,4,3:T(8,128)(2,1)} %bitcast.58) | data formatting | bytes 3145728 | tf_op jit(solution)/shard_map/all_to_all | solution.py:122
  146.7 4.7 %collective-permute-start.7 = (bf16[16,8,8,256]{3,0,2,1:T(8,128)(2,1)S(1)}, bf16[16,8,8,256]{3,0,2,1:T(8,128)(2,1)S(1)}, u32[]{:S(2)}, u32[]{:S(2)}) collective-permute-start(bf16[16,8,8,256]{3,0,2,1:T(8,128)(2,1)S(1)} %get-tuple-element.8), channel_id=1, source_target_pairs={{0,28},{4,0},{8,4},{12,8},{16,12},{20,16},{24,20},{28,24},{1,29},{... | collective-permute-start | bytes 1572872 | tf_op jit(solution)/shard_map/ppermute | solution.py:27
  152.7 2.1 %convolution_bitcast_fusion = f32[48,48]{1,0:T(8,128)S(1)} fusion(bf16[16,8,8,256]{3,0,2,1:T(8,128)(2,1)} %collective-permute-done.1, bf16[16,8,8,256]{3,0,2,1:T(8,128)(2,1)S(1)} %copy-done, bf16[16,8,8,256]{3,0,2,1:T(8,128)(2,1)} %collective-permute-done), kind=kOutput, calls=%fused_computation.38 | convolution fusion | flops 80216064 | bytes 1582080 | tf_op jit(solution)/shard_map/dot_general | solution.py:146
  154.8 4.7 %collective-permute-start.3 = (f32[16,48]{1,0:T(8,128)S(1)}, f32[16,48]{1,0:T(8,128)S(1)}, u32[]{:S(2)}, u32[]{:S(2)}) collective-permute-start(f32[16,48]{1,0:T(8,128)S(1)} %get-tuple-element.17), channel_id=1, source_target_pairs={{0,28},{4,0},{8,4},{12,8},{16,12},{20,16},{24,20},{28,24},{1,29},{... | collective-permute-start | bytes 9224 | tf_op jit(solution)/shard_map/ppermute | solution.py:27
  159.6 9.9 %collective-permute-done.6 = bf16[16,8,8,256]{3,0,2,1:T(8,128)(2,1)S(1)} collective-permute-done((bf16[16,8,8,256]{3,0,2,1:T(8,128)(2,1)}, bf16[16,8,8,256]{3,0,2,1:T(8,128)(2,1)S(1)}, u32[]{:S(2)}, u32[]{:S(2)}) %collective-permute-start.6) | collective-permute-done | bytes 524320 | tf_op jit(solution)/shard_map/ppermute | solution.py:27
  169.5 2.2 %collective-permute-done.7 = bf16[16,8,8,256]{3,0,2,1:T(8,128)(2,1)S(1)} collective-permute-done((bf16[16,8,8,256]{3,0,2,1:T(8,128)(2,1)S(1)}, bf16[16,8,8,256]{3,0,2,1:T(8,128)(2,1)S(1)}, u32[]{:S(2)}, u32[]{:S(2)}) %collective-permute-start.7) | collective-permute-done | bytes 524320 | tf_op jit(solution)/shard_map/ppermute | solution.py:27
  173.7 4.6 %collective-permute-start.9 = (f32[16,48]{1,0:T(8,128)S(1)}, f32[16,48]{1,0:T(8,128)S(1)}, u32[]{:S(2)}, u32[]{:S(2)}) collective-permute-start(f32[16,48]{1,0:T(8,128)S(1)} %get-tuple-element.14), channel_id=1, source_target_pairs={{0,28},{4,0},{8,4},{12,8},{16,12},{20,16},{24,20},{28,24},{1,29},{... | collective-permute-start | bytes 9224 | tf_op jit(solution)/shard_map/ppermute | solution.py:27
  180.0 10.1 %all-reduce.11 = (f32[16,80]{1,0:T(8,128)S(1)}, f32[16,80]{1,0:T(8,128)S(1)}) all-reduce(f32[16,80]{1,0:T(8,128)S(1)} %pad_add_fusion.1, f32[16,80]{1,0:T(8,128)S(1)} %pad_add_fusion), channel_id=2, replica_groups=mesh['slab'=8,'grp'=4] {'grp'}, use_global_device_ids=true, to_apply=%region_0.1.clone | all-reduce | flops 2560 | bytes 20480
  (41 shorter events, 14.1 us)
Async XLA Ops:
  0.6 45.1 %collective-permute-start.4 = (bf16[8,8,1024]{2,1,0:T(8,128)(2,1)}, bf16[8,8,1024]{2,1,0:T(8,128)(2,1)S(1)}, u32[]{:S(2)}, u32[]{:S(2)}) collective-permute-start(bf16[8,8,1024]{2,1,0:T(8,128)(2,1)} %param.4), channel_id=1, source_target_pairs={{0,4},{4,8},{8,12},{12,16},{16,20},{20,24},{24,28},{28,0},{1,5},{5... | collective-permute-start | bytes 393224 | tf_op jit(solution)/shard_map/ppermute | solution.py:18
  3.7 42.1 %collective-permute-start.5 = (bf16[8,8,1024]{2,1,0:T(8,128)(2,1)}, bf16[8,8,1024]{2,1,0:T(8,128)(2,1)S(1)}, u32[]{:S(2)}, u32[]{:S(2)}) collective-permute-start(bf16[8,8,1024]{2,1,0:T(8,128)(2,1)} %param.4), channel_id=1, source_target_pairs={{4,0},{8,4},{12,8},{16,12},{20,16},{24,20},{28,24},{0,28},{5,1},{9... | collective-permute-start | bytes 393224 | tf_op jit(solution)/shard_map/ppermute | solution.py:19
  35.5 45.1 %all-to-all-start = ((bf16[4,2,98304]{2,1,0:T(2,128)(2,1)}), bf16[4,2,98304]{2,1,0:T(2,128)(2,1)}, u32[]{:S(2)}, u32[]{:S(2)}) async-start(bf16[4,2,98304]{2,1,0:T(2,128)(2,1)} %reshape.116), calls=%async_computation | async-start | bytes 3145728 | tf_op jit(solution)/shard_map/all_to_all | solution.py:121
  45.2 0.9 copy-start.1
  80.6 38.9 %all-to-all-start.1 = ((bf16[4,2,98304]{2,1,0:T(2,128)(2,1)}), bf16[4,2,98304]{2,1,0:T(2,128)(2,1)S(1)}, u32[]{:S(2)}, u32[]{:S(2)}) async-start(bf16[4,2,98304]{2,1,0:T(2,128)(2,1)} %reshape.118), calls=%async_computation.1 | async-start | bytes 3145728 | tf_op jit(solution)/shard_map/all_to_all | solution.py:122
  114.8 37.8 %collective-permute-start = (bf16[16,8,8,256]{3,0,2,1:T(8,128)(2,1)}, bf16[16,8,8,256]{3,0,2,1:T(8,128)(2,1)}, u32[]{:S(2)}, u32[]{:S(2)}) collective-permute-start(bf16[16,8,8,256]{3,0,2,1:T(8,128)(2,1)} %get-tuple-element.10), channel_id=1, source_target_pairs={{0,4},{4,8},{8,12},{12,16},{16,20},{20,24},{24,28},{28,0},{1,5},{5... | collective-permute-start | bytes 1572872 | tf_op jit(solution)/shard_map/ppermute | solution.py:27
  114.8 37.8 %collective-permute-start.1 = (bf16[16,8,8,256]{3,0,2,1:T(8,128)(2,1)}, bf16[16,8,8,256]{3,0,2,1:T(8,128)(2,1)}, u32[]{:S(2)}, u32[]{:S(2)}) collective-permute-start(bf16[16,8,8,256]{3,0,2,1:T(8,128)(2,1)} %get-tuple-element.11), channel_id=1, source_target_pairs={{0,28},{4,0},{8,4},{12,8},{16,12},{20,16},{24,20},{28,24},{1,29},{... | collective-permute-start | bytes 1572872 | tf_op jit(solution)/shard_map/ppermute | solution.py:27
  145.7 5.7 %copy-start.2 = (u32[32]{0:T(128)S(1)}, u32[32]{0:T(128)}, u32[]{:S(2)}) copy-start(u32[32]{0:T(128)} %constant.181) | copy-start | bytes 388
  145.7 6.9 %copy-start = (bf16[16,8,8,256]{3,0,2,1:T(8,128)(2,1)S(1)}, bf16[16,8,8,256]{3,0,2,1:T(8,128)(2,1)}, u32[]{:S(2)}) copy-start(bf16[16,8,8,256]{3,0,2,1:T(8,128)(2,1)} %get-tuple-element.12) | copy-start | bytes 1572868
  146.7 22.8 %collective-permute-start.6 = (bf16[16,8,8,256]{3,0,2,1:T(8,128)(2,1)}, bf16[16,8,8,256]{3,0,2,1:T(8,128)(2,1)S(1)}, u32[]{:S(2)}, u32[]{:S(2)}) collective-permute-start(bf16[16,8,8,256]{3,0,2,1:T(8,128)(2,1)} %get-tuple-element.7), channel_id=1, source_target_pairs={{0,4},{4,8},{8,12},{12,16},{16,20},{20,24},{24,28},{28,0},{1,5},{5... | collective-permute-start | bytes 1572872 | tf_op jit(solution)/shard_map/ppermute | solution.py:27
  146.7 25.0 %collective-permute-start.7 = (bf16[16,8,8,256]{3,0,2,1:T(8,128)(2,1)S(1)}, bf16[16,8,8,256]{3,0,2,1:T(8,128)(2,1)S(1)}, u32[]{:S(2)}, u32[]{:S(2)}) collective-permute-start(bf16[16,8,8,256]{3,0,2,1:T(8,128)(2,1)S(1)} %get-tuple-element.8), channel_id=1, source_target_pairs={{0,28},{4,0},{8,4},{12,8},{16,12},{20,16},{24,20},{28,24},{1,29},{... | collective-permute-start | bytes 1572872 | tf_op jit(solution)/shard_map/ppermute | solution.py:27
  154.8 23.5 %collective-permute-start.2 = (f32[16,48]{1,0:T(8,128)S(1)}, f32[16,48]{1,0:T(8,128)S(1)}, u32[]{:S(2)}, u32[]{:S(2)}) collective-permute-start(f32[16,48]{1,0:T(8,128)S(1)} %get-tuple-element.18), channel_id=1, source_target_pairs={{0,4},{4,8},{8,12},{12,16},{16,20},{20,24},{24,28},{28,0},{1,5},{5... | collective-permute-start | bytes 9224 | tf_op jit(solution)/shard_map/ppermute | solution.py:27
  154.8 23.4 %collective-permute-start.3 = (f32[16,48]{1,0:T(8,128)S(1)}, f32[16,48]{1,0:T(8,128)S(1)}, u32[]{:S(2)}, u32[]{:S(2)}) collective-permute-start(f32[16,48]{1,0:T(8,128)S(1)} %get-tuple-element.17), channel_id=1, source_target_pairs={{0,28},{4,0},{8,4},{12,8},{16,12},{20,16},{24,20},{28,24},{1,29},{... | collective-permute-start | bytes 9224 | tf_op jit(solution)/shard_map/ppermute | solution.py:27
  173.5 6.4 %collective-permute-start.8 = (f32[16,48]{1,0:T(8,128)S(1)}, f32[16,48]{1,0:T(8,128)S(1)}, u32[]{:S(2)}, u32[]{:S(2)}) collective-permute-start(f32[16,48]{1,0:T(8,128)S(1)} %get-tuple-element.15), channel_id=1, source_target_pairs={{0,4},{4,8},{8,12},{12,16},{16,20},{20,24},{24,28},{28,0},{1,5},{5... | collective-permute-start | bytes 9224 | tf_op jit(solution)/shard_map/ppermute | solution.py:27
  173.7 6.2 %collective-permute-start.9 = (f32[16,48]{1,0:T(8,128)S(1)}, f32[16,48]{1,0:T(8,128)S(1)}, u32[]{:S(2)}, u32[]{:S(2)}) collective-permute-start(f32[16,48]{1,0:T(8,128)S(1)} %get-tuple-element.14), channel_id=1, source_target_pairs={{0,28},{4,0},{8,4},{12,8},{16,12},{20,16},{24,20},{28,24},{1,29},{... | collective-permute-start | bytes 9224 | tf_op jit(solution)/shard_map/ppermute | solution.py:27
where the time goes:
time: 192 us; the launch traced here: 191 us
  local copies, waits for them, and re-layouts  113 us (59%)
  starting transfers between devices  33.5 us (17%)
  matrix products  15.8 us (8%)
  waiting for transfers between devices  13.7 us (7%)
  blocking collectives  10.1 us (5%)
  other arithmetic  3.34 us (2%)
    unnamed x13, local copies, waits for them, and re-layouts  56.2 us
    convert_element_type x2, local copies, waits for them, and re-layouts, place_planes(): return placed.astype(jnp.bfloat16)  24.4 us
    ppermute x8, starting transfers between devices, shifted(): return lax.ppermute(value, axis, pairs)  19 us
    all_to_all x2, local copies, waits for them, and re-layouts, local(): lax.all_to_all(frame_orbital, 'grp', split_axis=3, concat_axis=0, tiled=T...  15.1 us
    ppermute x8, waiting for transfers between devices, shifted(): return lax.ppermute(value, axis, pairs)  13.7 us
    all_to_all x2, local copies, waits for them, and re-layouts, local(): lax.all_to_all(frame_applied, 'grp', split_axis=3, concat_axis=0, tiled=T...  12.8 us
    unnamed x1, blocking collectives  10.1 us
    dot_general x1, matrix products, apply_hamiltonian(): jnp.dot(orbital.reshape(-1, cell_count), laplace_plane(), preferred_eleme...  5.15 us
  transfers between devices with their start and end apart: 12, of which 3 were waited for; matrix products, arithmetic and copies ran while one was open for 67% of the time, Pallas kernels for 0%

commit v1 on v0

--- a/solution.py
+++ b/solution.py
@@ -6,6 +6,12 @@
 COMP = 8
 CX = 32
 CY = 32
+
+
+def exchange_blocks(x, axis, split, join):
+    cells = jnp.split(x, lax.axis_size(axis), axis=split)
+    got = lax.all_to_all(jnp.stack(cells), axis, 0, 0)
+    return jnp.concatenate(got, axis=join)
 
 
 def with_halo(value, sides, width):
@@ -119,7 +125,7 @@
     frame_applied = place_planes(frame_starts, frame_depth, applied)
     got_orbital, got_applied = (
         lax.all_to_all(frame_orbital, "grp", split_axis=3, concat_axis=0, tiled=True),
-        lax.all_to_all(frame_applied, "grp", split_axis=3, concat_axis=0, tiled=True),
+        exchange_blocks(frame_applied, "grp", 3, 0),
     )
     middle_orbital = got_orbital[:, rim_depth : rim_depth + slab_depth]
     middle_applied = got_applied[:, rim_depth : rim_depth + slab_depth]

time: 192 us -> 168 us (0.88)
  local copies, waits for them, and re-layouts: 113 us -> 62 us
  waiting for transfers between devices: 13.7 us -> 39.4 us
    unnamed x13 -> x14, local copies, waits for them, and re-layouts: 56.2 us -> 30.4 us
    ppermute x8, waiting for transfers between devices: 13.7 us -> 36.2 us  [shifted(): return lax.ppermute(value, axis, pairs)]
    all_to_all x2 -> x0, local copies, waits for them, and re-layouts: 12.8 us -> none  [local(): lax.all_to_all(frame_applied, 'grp', split_axis=3, concat_axis=0, tiled=T...]
    convert_element_type x2 -> x1, local copies, waits for them, and re-layouts: 24.4 us -> 12.2 us  [place_planes(): return placed.astype(jnp.bfloat16)]
    all_to_all x1, waiting for transfers between devices: 0.01 us -> 3.28 us  [local(): lax.all_to_all(frame_orbital, 'grp', split_axis=3, concat_axis=0, tiled=T...]
    ppermute x1, starting transfers between devices: 3.05 us -> 0.01 us  [with_halo(): before = lax.ppermute(last, axis, up)]
    ppermute x1, starting transfers between devices: 3.11 us -> 6.09 us  [with_halo(): after = lax.ppermute(initial, axis, down)]
  transfers between devices with their start and end apart: 12 -> 12, of which waited for: 3 -> 5; matrix products, arithmetic and copies ran while one was open for 67% -> 47% of each run, Pallas kernels for 0% -> 0%
where the time goes in v1:
time: 168 us; the launch traced here: 167 us
  local copies, waits for them, and re-layouts  62 us (37%)
  waiting for transfers between devices  39.4 us (23%)
  starting transfers between devices  33.6 us (20%)
  matrix products  15.6 us (9%)
  blocking collectives  10.1 us (6%)
  other arithmetic  4.75 us (3%)
    ppermute x8, waiting for transfers between devices, shifted(): return lax.ppermute(value, axis, pairs)  36.2 us
    unnamed x14, local copies, waits for them, and re-layouts  30.4 us
    ppermute x8, starting transfers between devices, shifted(): return lax.ppermute(value, axis, pairs)  19.4 us
    all_to_all x2, local copies, waits for them, and re-layouts, local(): lax.all_to_all(frame_orbital, 'grp', split_axis=3, concat_axis=0, tiled=T...  15.1 us
    convert_element_type x1, local copies, waits for them, and re-layouts, place_planes(): return placed.astype(jnp.bfloat16)  12.2 us
    unnamed x1, blocking collectives  10.1 us
    ppermute x1, starting transfers between devices, with_halo(): after = lax.ppermute(initial, axis, down)  6.09 us
    dot_general x1, matrix products, apply_hamiltonian(): jnp.dot(orbital.reshape(-1, cell_count), laplace_plane(), preferred_eleme...  5.15 us
  transfers between devices with their start and end apart: 12, of which 5 were waited for; matrix products, arithmetic and copies ran while one was open for 47% of the time, Pallas kernels for 0%

profile of v1, /device:TPU:0, one launch (start us, length us, event | category | flops | bytes accessed | tf_op | source)
XLA Modules:
  0.0 166.9 jit_solution(11768307259067228092)
XLA Ops:
  0.6 6.1 %collective-permute-start.5 = (bf16[8,8,1024]{2,1,0:T(8,128)(2,1)}, bf16[8,8,1024]{2,1,0:T(8,128)(2,1)S(1)}, u32[]{:S(2)}, u32[]{:S(2)}) collective-permute-start(bf16[8,8,1024]{2,1,0:T(8,128)(2,1)} %param.4), channel_id=1, source_target_pairs={{4,0},{8,4},{12,8},{16,12},{20,16},{24,20},{28,24},{0,28},{5,1},{9... | collective-permute-start | bytes 393224 | tf_op jit(solution)/shard_map/ppermute | solution.py:25
  7.6 1.4 broadcast_select_fusion
  10.0 12.2 %copy.13 = bf16[4,24,8,1024]{1,2,0,3:T(8,128)(2,1)} copy(bf16[4,24,8,1024]{3,1,2,0:T(8,128)(2,1)S(1)} %convolution_convert_fusion.1) | data formatting | bytes 3145728 | tf_op jit(solution)/shard_map/convert_element_type | solution.py:92
  22.2 13.3 %reshape.120 = bf16[4,2,98304]{2,1,0:T(2,128)(2,1)} reshape(bf16[1024,4,8,24]{3,2,1,0:T(8,128)(2,1)} %bitcast.58) | data formatting | bytes 3145728
  35.5 4.5 %all-to-all-start = ((bf16[4,2,98304]{2,1,0:T(2,128)(2,1)}), bf16[4,2,98304]{2,1,0:T(2,128)(2,1)}, u32[]{:S(2)}, u32[]{:S(2)}) async-start(bf16[4,2,98304]{2,1,0:T(2,128)(2,1)} %reshape.120), calls=%async_computation | async-start | bytes 3145728 | tf_op jit(solution)/shard_map/all_to_all | solution.py:127
  40.0 5.2 %fusion.2 = f32[4,16,8,1024]{3,2,1,0:T(8,128)} fusion(bf16[4,16,8,1024]{3,2,1,0:T(8,128)(2,1)S(1)} %broadcast_select_fusion, s32[1024]{0:T(1024)S(1)} %get-tuple-element.23, s32[1024]{0:T(1024)S(1)} %get-tuple-element.24), kind=kOutput, calls=%fused_computation.9 | convolution fusion | flops 1089470464 | bytes 3153920 | tf_op jit(solution)/shard_map/dot_general | solution.py:59
  47.0 2.7 %gather_fusion = bf16[4,16,8,1024]{3,2,1,0:T(8,128)(2,1)} fusion(bf16[40,8,1024]{2,1,0:T(8,128)(2,1)} %fusion.31, s32[4]{0:T(128)S(1)} %get-tuple-element.4), kind=kCustom, calls=%fused_computation | custom fusion | bytes 2097200 | tf_op jit(solution)/shard_map/vmap()/gather | solution.py:120
  49.7 4.4 %fusion.5 = bf16[4,16,8,1024]{3,2,1,0:T(8,128)(2,1)S(1)} fusion(f32[4,16,8,1024]{3,2,1,0:T(8,128)} %fusion.2, bf16[4,16,8,1024]{3,2,1,0:T(8,128)(2,1)S(1)} %broadcast_select_fusion, f32[4,16,1024,8]{2,3,1,0:T(8,128)S(1)} %fusion.59, bf16[4,16,8,1024]{3,2,1,0:T(8,128)(2,1)} %gather_fusion, pred[4,16]{1,0:T(4,128)(4,1)S(1)} %iota_compare_fusion.2), kind=kOutput, calls=%fused_computation.12 | convolution fusion | flops 57151744 | bytes 7340096 | tf_op jit(solution)/shard_map/kc,npkx->npcx/dot_general | solution.py:74
  55.3 1.4 pad_maximum_fusion.1
  56.7 3.3 %all-to-all-done = bf16[4,2,98304]{2,1,0:T(2,128)(2,1)} async-done(((bf16[4,2,98304]{2,1,0:T(2,128)(2,1)}), bf16[4,2,98304]{2,1,0:T(2,128)(2,1)}, u32[]{:S(2)}, u32[]{:S(2)}) %all-to-all-start) | async-done | bytes 1572896 | tf_op jit(solution)/shard_map/all_to_all | solution.py:127
  60.0 3.6 %all-to-all-start.1 = ((bf16[4,4,24,8,256]{4,2,3,1,0:T(8,128)(2,1)}), bf16[4,4,24,8,256]{4,2,3,1,0:T(8,128)(2,1)S(1)}, u32[]{:S(2)}, u32[]{:S(2)}) async-start(bf16[4,4,24,8,256]{4,2,3,1,0:T(8,128)(2,1)} %pad_maximum_fusion.1), calls=%async_computation.1 | async-start | bytes 3145728 | tf_op jit(solution)/shard_map/all_to_all | solution.py:13
  63.5 14.1 %reshape.121 = bf16[1024,4,8,24]{3,2,1,0:T(8,128)(2,1)} reshape(bf16[4,2,98304]{2,1,0:T(2,128)(2,1)} %all-to-all-done) | data formatting | bytes 3145728
  77.6 12.8 %copy.14 = bf16[4,24,8,4,256]{4,0,3,2,1:T(4,128)(2,1)} copy(bf16[4,24,8,4,256]{1,2,0,4,3:T(8,128)(2,1)} %bitcast.59) | data formatting | bytes 3145728 | tf_op jit(solution)/shard_map/all_to_all | solution.py:127
  90.4 2.4 %all_to_all.19 = bf16[16,24,8,256]{3,0,2,1:T(8,128)(2,1)S(1)} reshape(bf16[4,4,24,8,256]{4,1,0,3,2:T(4,128)(2,1)} %bitcast.61) | data formatting | bytes 3145728 | tf_op jit(solution)/shard_map/all_to_all | solution.py:127
  93.9 4.7 %collective-permute-start.1 = (bf16[16,8,8,256]{3,0,2,1:T(8,128)(2,1)}, bf16[16,8,8,256]{3,0,2,1:T(8,128)(2,1)S(1)}, u32[]{:S(2)}, u32[]{:S(2)}) collective-permute-start(bf16[16,8,8,256]{3,0,2,1:T(8,128)(2,1)} %get-tuple-element.15), channel_id=1, source_target_pairs={{0,28},{4,0},{8,4},{12,8},{16,12},{20,16},{24,20},{28,24},{1,29},{... | collective-permute-start | bytes 1572872 | tf_op jit(solution)/shard_map/ppermute | solution.py:33
  99.1 4.8 %collective-permute-start.7 = (bf16[16,8,8,256]{3,0,2,1:T(8,128)(2,1)S(1)}, bf16[16,8,8,256]{3,0,2,1:T(8,128)(2,1)}, u32[]{:S(2)}, u32[]{:S(2)}) collective-permute-start(bf16[16,8,8,256]{3,0,2,1:T(8,128)(2,1)S(1)} %copy.27), channel_id=1, source_target_pairs={{0,28},{4,0},{8,4},{12,8},{16,12},{20,16},{24,20},{28,24},{1,29},{... | collective-permute-start | bytes 1572872 | tf_op jit(solution)/shard_map/ppermute | solution.py:33
  105.8 25.6 %collective-permute-done.1 = bf16[16,8,8,256]{3,0,2,1:T(8,128)(2,1)S(1)} collective-permute-done((bf16[16,8,8,256]{3,0,2,1:T(8,128)(2,1)}, bf16[16,8,8,256]{3,0,2,1:T(8,128)(2,1)S(1)}, u32[]{:S(2)}, u32[]{:S(2)}) %collective-permute-start.1) | collective-permute-done | bytes 524320 | tf_op jit(solution)/shard_map/ppermute | solution.py:33
  131.4 1.7 %convolution_bitcast_fusion = f32[48,48]{1,0:T(8,128)S(1)} fusion(bf16[16,8,8,256]{3,0,2,1:T(8,128)(2,1)S(1)} %collective-permute-done.1, bf16[16,8,8,256]{3,0,2,1:T(8,128)(2,1)S(1)} %copy-done, bf16[16,8,8,256]{3,0,2,1:T(8,128)(2,1)} %collective-permute-done), kind=kOutput, calls=%fused_computation.39 | convolution fusion | flops 80216064 | bytes 1582080 | tf_op jit(solution)/shard_map/dot_general | solution.py:152
  133.2 4.9 %collective-permute-start.3 = (f32[16,48]{1,0:T(8,128)S(1)}, f32[16,48]{1,0:T(8,128)S(1)}, u32[]{:S(2)}, u32[]{:S(2)}) collective-permute-start(f32[16,48]{1,0:T(8,128)S(1)} %get-tuple-element.21), channel_id=1, source_target_pairs={{0,28},{4,0},{8,4},{12,8},{16,12},{20,16},{24,20},{28,24},{1,29},{... | collective-permute-start | bytes 9224 | tf_op jit(solution)/shard_map/ppermute | solution.py:33
  138.1 4.3 %collective-permute-done.7 = bf16[16,8,8,256]{3,0,2,1:T(8,128)(2,1)} collective-permute-done((bf16[16,8,8,256]{3,0,2,1:T(8,128)(2,1)S(1)}, bf16[16,8,8,256]{3,0,2,1:T(8,128)(2,1)}, u32[]{:S(2)}, u32[]{:S(2)}) %collective-permute-start.7) | collective-permute-done | bytes 524320 | tf_op jit(solution)/shard_map/ppermute | solution.py:33
  142.4 1.9 %fusion.25 = f32[48,48]{1,0:T(8,128)S(1)} fusion(bf16[16,8,8,256]{3,0,2,1:T(8,128)(2,1)} %collective-permute-done.7, bf16[16,8,8,256]{3,0,2,1:T(8,128)(2,1)S(1)} %copy.26, bf16[16,8,8,256]{3,0,2,1:T(8,128)(2,1)} %collective-permute-done.6, bf16[16,8,8,256]{3,0,2,1:T(8,128)(2,1)S(1)} %collective-permute-done.1, bf16[16,8,8,256]{3,0,2,1:T(8,128)(2,1)S(1)} %copy-done, ...), kind=kOutput, calls=%fused_computation.38 | convolution fusion | flops 84934656 | bytes 3154944 | tf_op jit(solution)/shard_map/dot_general | solution.py:155
  144.3 4.9 %collective-permute-start.9 = (f32[16,48]{1,0:T(8,128)S(1)}, f32[16,48]{1,0:T(8,128)S(1)}, u32[]{:S(2)}, u32[]{:S(2)}) collective-permute-start(f32[16,48]{1,0:T(8,128)S(1)} %get-tuple-element.18), channel_id=1, source_target_pairs={{0,28},{4,0},{8,4},{12,8},{16,12},{20,16},{24,20},{28,24},{1,29},{... | collective-permute-start | bytes 9224 | tf_op jit(solution)/shard_map/ppermute | solution.py:33
  150.6 5.0 %collective-permute-done.8 = f32[16,48]{1,0:T(8,128)S(1)} collective-permute-done((f32[16,48]{1,0:T(8,128)S(1)}, f32[16,48]{1,0:T(8,128)S(1)}, u32[]{:S(2)}, u32[]{:S(2)}) %collective-permute-start.8) | collective-permute-done | bytes 3104 | tf_op jit(solution)/shard_map/ppermute | solution.py:33
  155.6 10.1 %all-reduce.11 = (f32[16,80]{1,0:T(8,128)S(1)}, f32[16,80]{1,0:T(8,128)S(1)}) all-reduce(f32[16,80]{1,0:T(8,128)S(1)} %pad_add_fusion.1, f32[16,80]{1,0:T(8,128)S(1)} %pad_add_fusion), channel_id=2, replica_groups=mesh['slab'=8,'grp'=4] {'grp'}, use_global_device_ids=true, to_apply=%region_0.1.clone | all-reduce | flops 2560 | bytes 20480
  (41 shorter events, 10.3 us)
Async XLA Ops:
  0.6 45.0 %collective-permute-start.5 = (bf16[8,8,1024]{2,1,0:T(8,128)(2,1)}, bf16[8,8,1024]{2,1,0:T(8,128)(2,1)S(1)}, u32[]{:S(2)}, u32[]{:S(2)}) collective-permute-start(bf16[8,8,1024]{2,1,0:T(8,128)(2,1)} %param.4), channel_id=1, source_target_pairs={{4,0},{8,4},{12,8},{16,12},{20,16},{24,20},{28,24},{0,28},{5,1},{9... | collective-permute-start | bytes 393224 | tf_op jit(solution)/shard_map/ppermute | solution.py:25
  6.7 39.0 %collective-permute-start.4 = (bf16[8,8,1024]{2,1,0:T(8,128)(2,1)}, bf16[8,8,1024]{2,1,0:T(8,128)(2,1)S(1)}, u32[]{:S(2)}, u32[]{:S(2)}) collective-permute-start(bf16[8,8,1024]{2,1,0:T(8,128)(2,1)} %param.4), channel_id=1, source_target_pairs={{0,4},{4,8},{8,12},{12,16},{16,20},{20,24},{24,28},{28,0},{1,5},{5... | collective-permute-start | bytes 393224 | tf_op jit(solution)/shard_map/ppermute | solution.py:24
  35.5 24.5 %all-to-all-start = ((bf16[4,2,98304]{2,1,0:T(2,128)(2,1)}), bf16[4,2,98304]{2,1,0:T(2,128)(2,1)}, u32[]{:S(2)}, u32[]{:S(2)}) async-start(bf16[4,2,98304]{2,1,0:T(2,128)(2,1)} %reshape.120), calls=%async_computation | async-start | bytes 3145728 | tf_op jit(solution)/shard_map/all_to_all | solution.py:127
  45.2 0.9 copy-start.1
  60.0 38.7 %all-to-all-start.1 = ((bf16[4,4,24,8,256]{4,2,3,1,0:T(8,128)(2,1)}), bf16[4,4,24,8,256]{4,2,3,1,0:T(8,128)(2,1)S(1)}, u32[]{:S(2)}, u32[]{:S(2)}) async-start(bf16[4,4,24,8,256]{4,2,3,1,0:T(8,128)(2,1)} %pad_maximum_fusion.1), calls=%async_computation.1 | async-start | bytes 3145728 | tf_op jit(solution)/shard_map/all_to_all | solution.py:13
  93.9 37.5 %collective-permute-start.1 = (bf16[16,8,8,256]{3,0,2,1:T(8,128)(2,1)}, bf16[16,8,8,256]{3,0,2,1:T(8,128)(2,1)S(1)}, u32[]{:S(2)}, u32[]{:S(2)}) collective-permute-start(bf16[16,8,8,256]{3,0,2,1:T(8,128)(2,1)} %get-tuple-element.15), channel_id=1, source_target_pairs={{0,28},{4,0},{8,4},{12,8},{16,12},{20,16},{24,20},{28,24},{1,29},{... | collective-permute-start | bytes 1572872 | tf_op jit(solution)/shard_map/ppermute | solution.py:33
  98.7 32.8 %collective-permute-start = (bf16[16,8,8,256]{3,0,2,1:T(8,128)(2,1)}, bf16[16,8,8,256]{3,0,2,1:T(8,128)(2,1)}, u32[]{:S(2)}, u32[]{:S(2)}) collective-permute-start(bf16[16,8,8,256]{3,0,2,1:T(8,128)(2,1)} %get-tuple-element.14), channel_id=1, source_target_pairs={{0,4},{4,8},{8,12},{12,16},{16,20},{20,24},{24,28},{28,0},{1,5},{5... | collective-permute-start | bytes 1572872 | tf_op jit(solution)/shard_map/ppermute | solution.py:33
  98.7 5.6 %copy-start.2 = (u32[32]{0:T(128)S(1)}, u32[32]{0:T(128)}, u32[]{:S(2)}) copy-start(u32[32]{0:T(128)} %constant.181) | copy-start | bytes 388
  98.8 32.6 %copy-start = (bf16[16,8,8,256]{3,0,2,1:T(8,128)(2,1)S(1)}, bf16[16,8,8,256]{3,0,2,1:T(8,128)(2,1)}, u32[]{:S(2)}) copy-start(bf16[16,8,8,256]{3,0,2,1:T(8,128)(2,1)} %get-tuple-element.16) | copy-start | bytes 1572868
  99.1 43.2 %collective-permute-start.7 = (bf16[16,8,8,256]{3,0,2,1:T(8,128)(2,1)S(1)}, bf16[16,8,8,256]{3,0,2,1:T(8,128)(2,1)}, u32[]{:S(2)}, u32[]{:S(2)}) collective-permute-start(bf16[16,8,8,256]{3,0,2,1:T(8,128)(2,1)S(1)} %copy.27), channel_id=1, source_target_pairs={{0,28},{4,0},{8,4},{12,8},{16,12},{20,16},{24,20},{28,24},{1,29},{... | collective-permute-start | bytes 1572872 | tf_op jit(solution)/shard_map/ppermute | solution.py:33
  104.2 38.2 %collective-permute-start.6 = (bf16[16,8,8,256]{3,0,2,1:T(8,128)(2,1)S(1)}, bf16[16,8,8,256]{3,0,2,1:T(8,128)(2,1)}, u32[]{:S(2)}, u32[]{:S(2)}) collective-permute-start(bf16[16,8,8,256]{3,0,2,1:T(8,128)(2,1)S(1)} %copy.25), channel_id=1, source_target_pairs={{0,4},{4,8},{8,12},{12,16},{16,20},{20,24},{24,28},{28,0},{1,5},{5... | collective-permute-start | bytes 1572872 | tf_op jit(solution)/shard_map/ppermute | solution.py:33
  133.2 16.0 %collective-permute-start.3 = (f32[16,48]{1,0:T(8,128)S(1)}, f32[16,48]{1,0:T(8,128)S(1)}, u32[]{:S(2)}, u32[]{:S(2)}) collective-permute-start(f32[16,48]{1,0:T(8,128)S(1)} %get-tuple-element.21), channel_id=1, source_target_pairs={{0,28},{4,0},{8,4},{12,8},{16,12},{20,16},{24,20},{28,24},{1,29},{... | collective-permute-start | bytes 9224 | tf_op jit(solution)/shard_map/ppermute | solution.py:33
  138.1 11.2 %collective-permute-start.2 = (f32[16,48]{1,0:T(8,128)S(1)}, f32[16,48]{1,0:T(8,128)S(1)}, u32[]{:S(2)}, u32[]{:S(2)}) collective-permute-start(f32[16,48]{1,0:T(8,128)S(1)} %get-tuple-element.22), channel_id=1, source_target_pairs={{0,4},{4,8},{8,12},{12,16},{16,20},{20,24},{24,28},{28,0},{1,5},{5... | collective-permute-start | bytes 9224 | tf_op jit(solution)/shard_map/ppermute | solution.py:33
  144.3 6.3 %collective-permute-start.9 = (f32[16,48]{1,0:T(8,128)S(1)}, f32[16,48]{1,0:T(8,128)S(1)}, u32[]{:S(2)}, u32[]{:S(2)}) collective-permute-start(f32[16,48]{1,0:T(8,128)S(1)} %get-tuple-element.18), channel_id=1, source_target_pairs={{0,28},{4,0},{8,4},{12,8},{16,12},{20,16},{24,20},{28,24},{1,29},{... | collective-permute-start | bytes 9224 | tf_op jit(solution)/shard_map/ppermute | solution.py:33
  149.2 6.3 %collective-permute-start.8 = (f32[16,48]{1,0:T(8,128)S(1)}, f32[16,48]{1,0:T(8,128)S(1)}, u32[]{:S(2)}, u32[]{:S(2)}) collective-permute-start(f32[16,48]{1,0:T(8,128)S(1)} %get-tuple-element.19), channel_id=1, source_target_pairs={{0,4},{4,8},{8,12},{12,16},{16,20},{20,24},{24,28},{28,0},{1,5},{5... | collective-permute-start | bytes 9224 | tf_op jit(solution)/shard_map/ppermute | solution.py:33
